TPU v7x, 32 devices: a whole 2x2x4 slice. The times are simulated.
32 devices in a mesh: gx: 4 (over z), gy: 8 (over y, x, core).
Axes of the slice: x: 2, y: 2, z: 4, core: 2. Of those that a mesh axis runs over, the one named last changes fastest.
Arguments:
- features: bfloat16 [32768, 256], P(('gx', 'gy')), may hold values from -6 to 6
- self_weight_one: bfloat16 [256, 256], replicated, may hold values from -0.375 to 0.375
- neigh_weight_one: bfloat16 [256, 256], replicated, may hold values from -1.5 to 1.5
- self_weight_two: bfloat16 [256, 256], replicated, may hold values from -0.375 to 0.375
- neigh_weight_two: bfloat16 [256, 256], replicated, may hold values from -1.5 to 1.5
- degree: int32 [32768], P(('gx', 'gy')), may hold values from 128 to 383
- local_tiles: bfloat16 [1024, 128, 128], P(('gx', 'gy')), may hold values from 0 to 1, as said below
- local_coord: int32 [1024, 2], P(('gx', 'gy')), may hold values from 0 to 7, as said below
- local_count: int32 [32], P(('gx', 'gy')), may hold values from 1 to 32, as said below
- send_block: int32 [256], P(('gx', 'gy')), may hold values from 0 to 7
- boundary_tiles: bfloat16 [256, 128, 128], P(('gx', 'gy')), may hold values from 0 to 1, as said below
- boundary_row: int32 [256], P(('gx', 'gy')), may hold values from 0 to 7
- hub_rows: int32 [256], P(('gx', 'gy')), may hold values from 0 to 1023
- hub_tiles: bfloat16 [256, 128, 128], P(('gx', 'gy')), may hold values from 0 to 1, as said below
- hub_coord: int32 [256, 2], P(('gx', 'gy')), may hold values from 0 to 7, as said below
Outputs:
- node_out: bfloat16 [32768, 256], P(('gx', 'gy'))
Inputs may be any that keep to these rules, and one draw needn't show every extreme that they name: `local_tiles`: entries are 0 or 1. `boundary_tiles`: entries are 0 or 1. `hub_tiles`: entries are 0 or 1. `local_coord`: both columns are row blocks of the same device. `local_count`: some device has all 32 slots live. `hub_coord`: column 0 is a row block below 8, column 1 a hub block below 2.
All inputs are finite; a program needn't handle non-finite values.
Results may differ from a plain program's by a relative error of at most 0.005.
Values may be sent and summed in bfloat16 or wider, within the bound.
A program may use at most 64 MiB of HBM per device.

v0:
```python
import jax
import jax.numpy as jnp
from jax import lax
from jax.sharding import PartitionSpec as P


def tile_sum(tiles, rows, sources, weight, block_count):
    product = jnp.einsum("kij,kjf->kif", tiles, sources, preferred_element_type=jnp.float32)
    onehot = (rows[None, :] == jnp.arange(block_count, dtype=jnp.int32)[:, None]).astype(
        jnp.float32
    ) * weight[None, :]
    flat = product.reshape(product.shape[0], -1)
    merged = jnp.dot(onehot, flat, precision=lax.Precision.HIGHEST)
    return merged.reshape(block_count, product.shape[1], product.shape[2])


def layer(
    nodes_in,
    self_weight,
    neigh_weight,
    degree,
    local_tiles,
    local_coord,
    local_count,
    send_block,
    boundary_tiles,
    boundary_row,
    hub_rows,
    hub_tiles,
    hub_coord,
):
    node_count, feat_width = nodes_in.shape
    tile_size = local_tiles.shape[1]
    block_count = node_count // tile_size
    blocks = nodes_in.reshape(block_count, tile_size, feat_width)
    own_hubs = jnp.take(nodes_in, hub_rows, axis=0)
    inner = lax.all_gather(own_hubs, "gy", axis=0, tiled=True)
    hub_feats = lax.all_gather(inner, "gx", axis=0, tiled=True)
    outgoing = jnp.take(blocks, send_block, axis=0)
    incoming = lax.all_to_all(outgoing, "gy", split_axis=0, concat_axis=0, tiled=True)
    live_mask = (jnp.arange(local_tiles.shape[0], dtype=jnp.int32) < local_count[0]).astype(
        jnp.float32
    )
    sources = jnp.take(blocks, local_coord[:, 1], axis=0)
    totals = tile_sum(local_tiles, local_coord[:, 0], sources, live_mask, block_count)
    totals = totals + tile_sum(
        boundary_tiles,
        boundary_row,
        incoming,
        jnp.ones((boundary_tiles.shape[0],), jnp.float32),
        block_count,
    )
    hub_blocks = hub_feats.reshape(-1, tile_size, feat_width)
    hub_sources = jnp.take(hub_blocks, hub_coord[:, 1], axis=0)
    totals = totals + tile_sum(
        hub_tiles,
        hub_coord[:, 0],
        hub_sources,
        jnp.ones((hub_tiles.shape[0],), jnp.float32),
        block_count,
    )
    neigh = (totals.reshape(node_count, feat_width) / degree[:, None].astype(jnp.float32)).astype(
        jnp.bfloat16
    )
    linear = jnp.dot(nodes_in, self_weight, preferred_element_type=jnp.float32)
    return linear + jnp.dot(neigh, neigh_weight, preferred_element_type=jnp.float32)


def per_device(
    features,
    self_weight_one,
    neigh_weight_one,
    self_weight_two,
    neigh_weight_two,
    degree,
    local_tiles,
    local_coord,
    local_count,
    send_block,
    boundary_tiles,
    boundary_row,
    hub_rows,
    hub_tiles,
    hub_coord,
):
    graph = (
        degree,
        local_tiles,
        local_coord,
        local_count,
        send_block,
        boundary_tiles,
        boundary_row,
        hub_rows,
        hub_tiles,
        hub_coord,
    )
    linear_one = layer(features, self_weight_one, neigh_weight_one, *graph)
    relu_one = jnp.maximum(linear_one, 0.0)
    scale = lax.rsqrt(jnp.mean(relu_one * relu_one, axis=-1, keepdims=True) + 1e-06)
    hidden = (relu_one * scale).astype(jnp.bfloat16)
    linear_two = layer(hidden, self_weight_two, neigh_weight_two, *graph)
    return linear_two.astype(jnp.bfloat16)


def solution(mesh):
    placed = (
        P(("gx", "gy"), None),
        P(),
        P(),
        P(),
        P(),
        P(("gx", "gy")),
        P(("gx", "gy"), None, None),
        P(("gx", "gy"), None),
        P(("gx", "gy")),
        P(("gx", "gy")),
        P(("gx", "gy"), None, None),
        P(("gx", "gy")),
        P(("gx", "gy")),
        P(("gx", "gy"), None, None),
        P(("gx", "gy"), None),
    )
    return jax.shard_map(
        per_device, mesh=mesh, in_specs=placed, out_specs=P(("gx", "gy"), None), check_vma=False
    )
```

profile of v0, /device:TPU:0, one launch (start us, length us, event | category | flops | bytes accessed | tf_op | source)
XLA Modules:
  0.0 126.4 jit_solution(13274462036618419214)
XLA Ops:
  0.0 0.8 compare_select_fusion.2
  0.8 0.7 compare_and_fusion.2
  1.5 1.6 %gather_fusion.1 = bf16[8,128,256]{2,1,0:T(8,128)(2,1)S(1)} fusion(bf16[8,128,256]{2,1,0:T(8,128)(2,1)} %bitcast.127, s32[1024]{0:T(1024)S(1)} %pad_clamp_fusion.2), kind=kCustom, calls=%fused_computation.1.clone | custom fusion | bytes 1048608 | tf_op jit(solution)/shard_map/jit(_take)/gather | solution.py:39
  3.1 0.3 copy.19
  3.4 0.9 broadcast_select_fusion.1
  4.3 5.2 %all-to-all-start = ((bf16[8,128,256]{1,2,0:T(8,128)(2,1)}), bf16[8,128,256]{1,2,0:T(8,128)(2,1)S(1)}, u32[]{:S(2)}, u32[]{:S(2)}) async-start(bf16[8,128,256]{1,2,0:T(8,128)(2,1)} %broadcast_select_fusion.1), calls=%async_computation | async-start | bytes 1048576 | tf_op jit(solution)/shard_map/all_to_all | solution.py:40
  9.5 0.6 slice_bitcast_fusion.1
  10.1 2.0 %gather_fusion = bf16[32,128,256]{2,1,0:T(8,128)(2,1)} fusion(bf16[8,128,256]{2,1,0:T(8,128)(2,1)S(1)} %bitcast.128, s32[1024]{0:T(1024)S(1)} %pad_clamp_fusion.3), kind=kCustom, calls=%fused_computation.clone | custom fusion | bytes 4194432 | tf_op jit(solution)/shard_map/jit(_take)/gather | solution.py:44
  12.2 4.4 %convolution_bitcast_fusion.1 = f32[32,128,256]{1,2,0:T(8,128)} fusion(bf16[32,128,128]{2,1,0:T(8,128)(2,1)S(1)} %copy-done, bf16[32,128,256]{2,1,0:T(8,128)(2,1)} %gather_fusion, pred[32]{0:T(512)(128)(4,1)S(1)} %get-tuple-element.10), kind=kOutput, calls=%fused_computation.15 | convolution fusion | flops 269484032 | bytes 7340064 | tf_op jit(solution)/shard_map/kij,kjf->kif/dot_general | solution.py:8
  16.6 5.4 %copy.38 = f32[4,8,128,256]{3,1,2,0:T(8,128)} copy(f32[4,8,128,256]{2,3,1,0:T(8,128)} %bitcast.130) | data formatting | bytes 8388608
  22.7 0.5 compare_convert_fusion
  23.3 0.6 gather_fusion.2
  23.9 9.6 %all_gather.12 = bf16[64,256]{1,0:T(8,128)(2,1)S(1)} all-gather(bf16[8,256]{1,0:T(8,128)(2,1)S(1)} %broadcast_select_fusion.3), channel_id=1, replica_groups=mesh['gx'=4,'gy'=8] {'gy'}, dimensions={0}, use_global_device_ids=true | all-gather | bytes 36864 | tf_op jit(solution)/shard_map/all_gather | solution.py:37
  33.5 13.6 %all_gather.13 = bf16[256,256]{1,0:T(8,128)(2,1)S(1)} all-gather(bf16[64,256]{1,0:T(8,128)(2,1)S(1)} %all_gather.12), channel_id=1, replica_groups=mesh['gx'=4,'gy'=8] {'gx'}, dimensions={0}, use_global_device_ids=true | all-gather | bytes 163840 | tf_op jit(solution)/shard_map/all_gather | solution.py:38
  47.1 0.5 compare_and_fusion
  47.6 1.4 %gather_fusion.3 = bf16[8,128,256]{2,1,0:T(8,128)(2,1)} fusion(bf16[2,128,256]{2,1,0:T(8,128)(2,1)S(1)} %bitcast.135, s32[1024]{0:T(1024)S(1)} %pad_clamp_fusion), kind=kCustom, calls=%fused_computation.3.clone | custom fusion | bytes 1048608 | tf_op jit(solution)/shard_map/jit(_take)/gather | solution.py:54
  49.0 1.5 %convolution_bitcast_fusion.4 = f32[8,128,256]{1,2,0:T(8,128)S(1)} fusion(bf16[8,128,128]{2,1,0:T(8,128)(2,1)} %param.36, bf16[8,128,256]{2,1,0:T(8,128)(2,1)} %gather_fusion.3, pred[8]{0:T(512)(128)(4,1)} %get-tuple-element.6), kind=kOutput, calls=%fused_computation.27 | convolution fusion | flops 67371008 | bytes 1835016 | tf_op jit(solution)/shard_map/kij,kjf->kif/dot_general | solution.py:8
  50.6 1.4 %copy.22 = f32[8,128,256]{2,1,0:T(8,128)} copy(f32[8,128,256]{1,2,0:T(8,128)S(1)} %convolution_bitcast_fusion.4) | data formatting | bytes 2097152 | tf_op jit(solution)/shard_map/kij,kjf->kif/dot_general | solution.py:8
  51.9 0.7 convert_element_type.32
  52.6 1.2 slice_bitcast_fusion
  53.8 1.3 %fusion.64 = f32[1024,256]{1,0:T(8,128)} fusion(bf16[1024,256]{1,0:T(8,128)(2,1)S(1)} %copy-done.1, bf16[256,256]{1,0:T(8,128)(2,1)S(1)} %copy-done.8), kind=kOutput, calls=%fused_computation.101 | convolution fusion | flops 134217728 | bytes 1703936 | tf_op jit(solution)/shard_map/dot_general | solution.py:65
  55.1 0.3 convolution_bitcast_fusion.5
  55.4 1.3 %copy.20 = f32[8,128,256]{2,1,0:T(8,128)} copy(f32[8,128,256]{1,2,0:T(8,128)S(1)} %convolution_bitcast_fusion.5) | data formatting | bytes 2097152 | tf_op jit(solution)/shard_map/kij,kjf->kif/dot_general | solution.py:8
  56.7 2.5 %fusion.35 = f32[8,128,256]{2,0,1:T(8,128)S(1)} fusion(s32[8]{0:T(128)} %param.34, f32[1,8,128,256]{3,2,1,0:T(8,128)} %bitcast.131), kind=kOutput, calls=%fused_computation.64 | convolution fusion | flops 25165888 | bytes 2097184 | tf_op jit(solution)/shard_map/dot_general | solution.py:13
  59.2 3.8 %fusion.10 = f32[8,128,256]{2,0,1:T(8,128)S(1)} fusion(f32[8,128,256]{2,0,1:T(8,128)S(1)} %fusion.35, f32[32]{0:T(128)S(1)} %copy-done.21, s32[32]{0:T(128)S(1)} %copy-done.19, f32[4,8,128,256]{3,1,2,0:T(8,128)} %copy.38), kind=kOutput, calls=%fused_computation.20 | convolution fusion | flops 100925952 | bytes 6291712 | tf_op jit(solution)/shard_map/dot_general | solution.py:13
  63.1 1.2 convolution_add_fusion.3
  64.3 0.3 copy.23
  64.9 0.4 multiply_reduce_fusion
  65.5 2.0 %gather_fusion.4 = bf16[32,128,256]{2,1,0:T(8,128)(2,1)} fusion(bf16[8,128,256]{2,1,0:T(8,128)(2,1)S(1)} %bitcast.125, s32[1024]{0:T(1024)S(1)} %pad_clamp_fusion.3), kind=kCustom, calls=%fused_computation.4.clone | custom fusion | bytes 4194432 | tf_op jit(solution)/shard_map/jit(_take)/gather | solution.py:44
  67.5 0.6 gather_fusion.5
  68.1 0.7 gather_fusion.6
  68.8 4.4 %convolution_bitcast_fusion = f32[32,128,256]{1,2,0:T(8,128)} fusion(bf16[32,128,128]{2,1,0:T(8,128)(2,1)S(1)} %copy-done, bf16[32,128,256]{2,1,0:T(8,128)(2,1)} %gather_fusion.4, pred[32]{0:T(512)(128)(4,1)S(1)} %copy-done.24), kind=kOutput, calls=%fused_computation.14 | convolution fusion | flops 269484032 | bytes 7340064 | tf_op jit(solution)/shard_map/kij,kjf->kif/dot_general | solution.py:8
  73.3 5.4 %copy.41 = f32[4,8,128,256]{3,1,2,0:T(8,128)} copy(f32[4,8,128,256]{2,3,1,0:T(8,128)} %bitcast.129) | data formatting | bytes 8388608
  79.0 0.9 broadcast_select_fusion
  79.9 3.5 %all-to-all-start.1 = ((bf16[8,128,256]{1,2,0:T(8,128)(2,1)}), bf16[8,128,256]{1,2,0:T(8,128)(2,1)S(1)}, u32[]{:S(2)}, u32[]{:S(2)}) async-start(bf16[8,128,256]{1,2,0:T(8,128)(2,1)} %broadcast_select_fusion), calls=%async_computation.1 | async-start | bytes 1048576 | tf_op jit(solution)/shard_map/all_to_all | solution.py:40
  83.5 12.9 %all_gather.14 = bf16[64,256]{1,0:T(8,128)(2,1)S(1)} all-gather(bf16[8,256]{1,0:T(8,128)(2,1)S(1)} %broadcast_select_fusion.2), channel_id=1, replica_groups=mesh['gx'=4,'gy'=8] {'gy'}, dimensions={0}, use_global_device_ids=true | all-gather | bytes 36864 | tf_op jit(solution)/shard_map/all_gather | solution.py:37
  96.3 13.6 %all_gather.15 = bf16[256,256]{1,0:T(8,128)(2,1)S(1)} all-gather(bf16[64,256]{1,0:T(8,128)(2,1)S(1)} %all_gather.14), channel_id=1, replica_groups=mesh['gx'=4,'gy'=8] {'gx'}, dimensions={0}, use_global_device_ids=true | all-gather | bytes 163840 | tf_op jit(solution)/shard_map/all_gather | solution.py:38
  109.9 1.4 %gather_fusion.7 = bf16[8,128,256]{2,1,0:T(8,128)(2,1)} fusion(bf16[2,128,256]{2,1,0:T(8,128)(2,1)S(1)} %bitcast.136, s32[1024]{0:T(1024)S(1)} %pad_clamp_fusion), kind=kCustom, calls=%fused_computation.7.clone | custom fusion | bytes 1048608 | tf_op jit(solution)/shard_map/jit(_take)/gather | solution.py:54
  111.3 1.5 %convolution_bitcast_fusion.2 = f32[8,128,256]{1,2,0:T(8,128)S(1)} fusion(bf16[8,128,128]{2,1,0:T(8,128)(2,1)} %param.36, bf16[8,128,256]{2,1,0:T(8,128)(2,1)} %gather_fusion.7, pred[8]{0:T(512)(128)(4,1)} %get-tuple-element.6), kind=kOutput, calls=%fused_computation.23 | convolution fusion | flops 67371008 | bytes 1835016 | tf_op jit(solution)/shard_map/kij,kjf->kif/dot_general | solution.py:8
  112.8 1.3 %copy.30 = f32[8,128,256]{2,1,0:T(8,128)} copy(f32[8,128,256]{1,2,0:T(8,128)S(1)} %convolution_bitcast_fusion.2) | data formatting | bytes 2097152 | tf_op jit(solution)/shard_map/kij,kjf->kif/dot_general | solution.py:8
  114.2 1.3 %fusion.65 = f32[1024,256]{1,0:T(8,128)} fusion(bf16[1024,256]{1,0:T(8,128)(2,1)S(1)} %multiply_convert_fusion, bf16[256,256]{1,0:T(8,128)(2,1)S(1)} %copy-done.9), kind=kOutput, calls=%fused_computation.102 | convolution fusion | flops 134217728 | bytes 1703936 | tf_op jit(solution)/shard_map/dot_general | solution.py:65
  115.5 0.3 convolution_bitcast_fusion.3
  115.8 1.3 %copy.28 = f32[8,128,256]{2,1,0:T(8,128)} copy(f32[8,128,256]{1,2,0:T(8,128)S(1)} %convolution_bitcast_fusion.3) | data formatting | bytes 2097152 | tf_op jit(solution)/shard_map/kij,kjf->kif/dot_general | solution.py:8
  117.1 2.5 %fusion.33 = f32[8,128,256]{2,0,1:T(8,128)S(1)} fusion(s32[8]{0:T(128)S(1)} %copy-done.12, f32[1,8,128,256]{3,2,1,0:T(8,128)} %bitcast.132), kind=kOutput, calls=%fused_computation.63 | convolution fusion | flops 25165888 | bytes 2097184 | tf_op jit(solution)/shard_map/dot_general | solution.py:13
  119.6 3.8 %fusion.13 = f32[8,128,256]{2,0,1:T(8,128)S(1)} fusion(f32[8,128,256]{2,0,1:T(8,128)S(1)} %fusion.33, f32[32]{0:T(128)S(1)} %copy-done.22, s32[32]{0:T(128)S(1)} %copy-done.20, f32[4,8,128,256]{3,1,2,0:T(8,128)} %copy.41), kind=kOutput, calls=%fused_computation.21 | convolution fusion | flops 100925952 | bytes 6291712 | tf_op jit(solution)/shard_map/dot_general | solution.py:13
  123.5 1.2 convolution_add_fusion.2
  124.7 0.3 copy.31
  125.3 1.1 fusion.17
  (72 shorter events, 1.2 us)
Async XLA Ops:
  0.0 12.2 %copy-start = (bf16[32,128,128]{2,1,0:T(8,128)(2,1)S(1)}, bf16[32,128,128]{2,1,0:T(8,128)(2,1)}, u32[]{:S(2)}) copy-start(bf16[32,128,128]{2,1,0:T(8,128)(2,1)} %param.29) | copy-start | bytes 3145732
  0.0 10.1 %copy-start.1 = (bf16[1024,256]{1,0:T(8,128)(2,1)S(1)}, bf16[1024,256]{1,0:T(8,128)(2,1)}, u32[]{:S(2)}) copy-start(bf16[1024,256]{1,0:T(8,128)(2,1)} %param.23) | copy-start | bytes 1572868
  0.0 9.5 %copy-start.25 = (s32[32,2]{0,1:T(2,128)S(1)}, s32[32,2]{0,1:T(2,128)}, u32[]{:S(2)}) copy-start(s32[32,2]{0,1:T(2,128)} %param.30) | copy-start | bytes 772
  0.0 10.1 %copy-start.27 = (s32[8]{0:T(128)S(1)}, s32[8]{0:T(128)}, u32[]{:S(2)}) copy-start(s32[8]{0:T(128)} %param.35) | copy-start | bytes 100
  1.5 2.8 %copy-start.13 = (pred[8]{0:T(512)(128)(4,1)}, pred[8]{0:T(512)(128)(4,1)S(1)}, u32[]{:S(2)}) copy-start(pred[8]{0:T(512)(128)(4,1)S(1)} %compare_and_fusion.2) | copy-start | bytes 28
  4.3 50.8 %all-to-all-start = ((bf16[8,128,256]{1,2,0:T(8,128)(2,1)}), bf16[8,128,256]{1,2,0:T(8,128)(2,1)S(1)}, u32[]{:S(2)}, u32[]{:S(2)}) async-start(bf16[8,128,256]{1,2,0:T(8,128)(2,1)} %broadcast_select_fusion.1), calls=%async_computation | async-start | bytes 1048576 | tf_op jit(solution)/shard_map/all_to_all | solution.py:40
  9.5 7.1 %copy-start.23 = (pred[32]{0:T(512)(128)(4,1)}, pred[32]{0:T(512)(128)(4,1)S(1)}, u32[]{:S(2)}) copy-start(pred[32]{0:T(512)(128)(4,1)S(1)} %get-tuple-element.10) | copy-start | bytes 100
  10.1 13.8 %copy-start.15 = (pred[8]{0:T(512)(128)(4,1)}, pred[8]{0:T(512)(128)(4,1)S(1)}, u32[]{:S(2)}) copy-start(pred[8]{0:T(512)(128)(4,1)S(1)} %compare_and_fusion.1) | copy-start | bytes 28
  16.6 30.5 %copy-start.26 = (s32[8,2]{0,1:T(2,128)S(1)}, s32[8,2]{0,1:T(2,128)}, u32[]{:S(2)}) copy-start(s32[8,2]{0,1:T(2,128)} %param.37) | copy-start | bytes 196
  22.0 31.7 %copy-start.8 = (bf16[256,256]{1,0:T(8,128)(2,1)S(1)}, bf16[256,256]{1,0:T(8,128)(2,1)}, u32[]{:S(2)}) copy-start(bf16[256,256]{1,0:T(8,128)(2,1)} %param.24) | copy-start | bytes 393220
  22.0 33.0 %copy-start.6 = (bf16[8,128,128]{2,1,0:T(8,128)(2,1)S(1)}, bf16[8,128,128]{2,1,0:T(8,128)(2,1)}, u32[]{:S(2)}) copy-start(bf16[8,128,128]{2,1,0:T(8,128)(2,1)} %param.33) | copy-start | bytes 786436
  23.3 27.3 %copy-start.11 = (s32[1024]{0:T(1024)}, s32[1024]{0:T(1024)S(1)}, u32[]{:S(2)}) copy-start(s32[1024]{0:T(1024)S(1)} %pad_clamp_fusion.1) | copy-start | bytes 12292
  55.0 4.1 %copy-start.19 = (s32[32]{0:T(128)S(1)}, s32[32]{0:T(128)}, u32[]{:S(2)}) copy-start(s32[32]{0:T(128)} %slice_bitcast_fusion.1) | copy-start | bytes 388
  55.0 4.1 %copy-start.21 = (f32[32]{0:T(128)S(1)}, f32[32]{0:T(128)}, u32[]{:S(2)}) copy-start(f32[32]{0:T(128)} %compare_convert_fusion) | copy-start | bytes 388
  56.7 6.4 %copy-start.3 = (f32[8,128,256]{2,1,0:T(8,128)S(1)}, f32[8,128,256]{2,1,0:T(8,128)}, u32[]{:S(2)}) copy-start(f32[8,128,256]{2,1,0:T(8,128)} %copy.22) | copy-start | bytes 3145732
  56.7 6.4 %copy-start.17 = (s32[8]{0:T(128)S(1)}, s32[8]{0:T(128)}, u32[]{:S(2)}) copy-start(s32[8]{0:T(128)} %slice_bitcast_fusion) | copy-start | bytes 100
  63.0 1.8 %copy-start.5 = (f32[1024,256]{1,0:T(8,128)S(1)}, f32[1024,256]{1,0:T(8,128)}, u32[]{:S(2)}) copy-start(f32[1024,256]{1,0:T(8,128)} %fusion.64) | copy-start | bytes 3145732
  63.0 1.8 %copy-start.10 = (bf16[256,256]{1,0:T(8,128)(2,1)S(1)}, bf16[256,256]{1,0:T(8,128)(2,1)}, u32[]{:S(2)}) copy-start(bf16[256,256]{1,0:T(8,128)(2,1)} %param.25) | copy-start | bytes 393220
  64.9 4.0 %copy-start.24 = (pred[32]{0:T(512)(128)(4,1)S(1)}, pred[32]{0:T(512)(128)(4,1)}, u32[]{:S(2)}) copy-start(pred[32]{0:T(512)(128)(4,1)} %copy-done.23) | copy-start | bytes 100
  73.3 5.7 %copy-start.14 = (pred[8]{0:T(512)(128)(4,1)S(1)}, pred[8]{0:T(512)(128)(4,1)}, u32[]{:S(2)}) copy-start(pred[8]{0:T(512)(128)(4,1)} %copy-done.13) | copy-start | bytes 28
  73.3 10.1 %copy-start.16 = (pred[8]{0:T(512)(128)(4,1)S(1)}, pred[8]{0:T(512)(128)(4,1)}, u32[]{:S(2)}) copy-start(pred[8]{0:T(512)(128)(4,1)} %copy-done.15) | copy-start | bytes 28
  78.7 35.5 %copy-start.9 = (bf16[256,256]{1,0:T(8,128)(2,1)S(1)}, bf16[256,256]{1,0:T(8,128)(2,1)}, u32[]{:S(2)}) copy-start(bf16[256,256]{1,0:T(8,128)(2,1)} %param.26) | copy-start | bytes 393220
  79.9 35.6 %all-to-all-start.1 = ((bf16[8,128,256]{1,2,0:T(8,128)(2,1)}), bf16[8,128,256]{1,2,0:T(8,128)(2,1)S(1)}, u32[]{:S(2)}, u32[]{:S(2)}) async-start(bf16[8,128,256]{1,2,0:T(8,128)(2,1)} %broadcast_select_fusion), calls=%async_computation.1 | async-start | bytes 1048576 | tf_op jit(solution)/shard_map/all_to_all | solution.py:40
  112.8 4.3 %copy-start.12 = (s32[8]{0:T(128)S(1)}, s32[8]{0:T(128)}, u32[]{:S(2)}) copy-start(s32[8]{0:T(128)} %param.34) | copy-start | bytes 100
  114.2 5.4 %copy-start.20 = (s32[32]{0:T(128)S(1)}, s32[32]{0:T(128)}, u32[]{:S(2)}) copy-start(s32[32]{0:T(128)} %slice_bitcast_fusion.1) | copy-start | bytes 388
  114.2 5.4 %copy-start.22 = (f32[32]{0:T(128)S(1)}, f32[32]{0:T(128)}, u32[]{:S(2)}) copy-start(f32[32]{0:T(128)} %compare_convert_fusion) | copy-start | bytes 388
  117.1 6.4 %copy-start.2 = (f32[8,128,256]{2,1,0:T(8,128)S(1)}, f32[8,128,256]{2,1,0:T(8,128)}, u32[]{:S(2)}) copy-start(f32[8,128,256]{2,1,0:T(8,128)} %copy.30) | copy-start | bytes 3145732
  117.1 6.4 %copy-start.18 = (s32[8]{0:T(128)S(1)}, s32[8]{0:T(128)}, u32[]{:S(2)}) copy-start(s32[8]{0:T(128)} %slice_bitcast_fusion) | copy-start | bytes 100
  123.4 1.8 %copy-start.4 = (f32[1024,256]{1,0:T(8,128)S(1)}, f32[1024,256]{1,0:T(8,128)}, u32[]{:S(2)}) copy-start(f32[1024,256]{1,0:T(8,128)} %fusion.65) | copy-start | bytes 3145732
  123.5 1.8 %copy-start.7 = (bf16[256,256]{1,0:T(8,128)(2,1)S(1)}, bf16[256,256]{1,0:T(8,128)(2,1)}, u32[]{:S(2)}) copy-start(bf16[256,256]{1,0:T(8,128)(2,1)} %param.27) | copy-start | bytes 393220
where the time goes:
time: 127 us; the launch traced here: 126 us
  blocking collectives  49.6 us (39%)
  matrix products  31.6 us (25%)
  local copies, waits for them, and re-layouts  29.5 us (23%)
  starting transfers between devices  8.67 us (7%)
  other arithmetic  5.83 us (5%)
    all_gather x2, blocking collectives, layer(): hub_feats = lax.all_gather(inner, 'gx', axis=0, tiled=True)  27.1 us
    all_gather x2, blocking collectives, layer(): inner = lax.all_gather(own_hubs, 'gy', axis=0, tiled=True)  22.4 us
    dot_general x6, matrix products, tile_sum(): merged = jnp.dot(onehot, flat, precision=lax.Precision.HIGHEST)  15 us
    dot_general x6, matrix products, tile_sum(): jnp.einsum('kij,kjf->kif', tiles, sources, preferred_element_type=jnp.flo...  12.5 us
    unnamed x58, local copies, waits for them, and re-layouts  11 us
    all_to_all x2, starting transfers between devices, layer(): lax.all_to_all(outgoing, 'gy', split_axis=0, concat_axis=0, tiled=True)  8.67 us
    dot_general x4, local copies, waits for them, and re-layouts, tile_sum(): jnp.einsum('kij,kjf->kif', tiles, sources, preferred_element_type=jnp.flo...  5.27 us
    gather x2, local copies, waits for them, and re-layouts, layer(): sources = jnp.take(blocks, local_coord[:, 1], axis=0)  4.08 us
  transfers between devices with their start and end apart: 2, of which 0 were waited for; matrix products, arithmetic and copies ran while one was open for 22% of the time, Pallas kernels for 0%

commit v1 on v0

--- a/solution.py
+++ b/solution.py
@@ -35,7 +35,14 @@
     blocks = nodes_in.reshape(block_count, tile_size, feat_width)
     own_hubs = jnp.take(nodes_in, hub_rows, axis=0)
     inner = lax.all_gather(own_hubs, "gy", axis=0, tiled=True)
-    hub_feats = lax.all_gather(inner, "gx", axis=0, tiled=True)
+    ways, here, step = (lax.axis_size("gx"), lax.axis_index("gx"), inner.shape[0])
+    line, have = (inner, 1)
+    while have < ways:
+        line = jnp.concatenate(
+            [line, lax.ppermute(line, "gx", [(d, (d - have) % ways) for d in range(ways)])], axis=0
+        )
+        have = 2 * have
+    hub_feats = jnp.roll(line, here * step, axis=0)
     outgoing = jnp.take(blocks, send_block, axis=0)
     incoming = lax.all_to_all(outgoing, "gy", split_axis=0, concat_axis=0, tiled=True)
     live_mask = (jnp.arange(local_tiles.shape[0], dtype=jnp.int32) < local_count[0]).astype(

time: 127 us -> 99.5 us (0.78)
  blocking collectives: 49.6 us -> 19.9 us
  waiting for transfers between devices: 0.01 us -> 5.27 us
  local copies, waits for them, and re-layouts: 29.5 us -> 25.3 us
  starting transfers between devices: 8.67 us -> 12.7 us
  matrix products: 31.6 us -> 28.8 us
    all_gather x2 -> x0, blocking collectives: 27.1 us -> none  [layer(): hub_feats = lax.all_gather(inner, 'gx', axis=0, tiled=True)]
    ppermute x0 -> x4, starting transfers between devices: none -> 5.51 us  [layer(): lax.ppermute(line, 'gx', [(d, (d - have) % ways) for d in range(ways)])]
    ppermute x0 -> x4, waiting for transfers between devices: none -> 5.27 us  [layer(): lax.ppermute(line, 'gx', [(d, (d - have) % ways) for d in range(ways)])]
    dot_general x6, matrix products: 15 us -> 12.4 us  [tile_sum(): merged = jnp.dot(onehot, flat, precision=lax.Precision.HIGHEST)]
    all_gather x2, blocking collectives: 22.4 us -> 19.9 us  [layer(): inner = lax.all_gather(own_hubs, 'gy', axis=0, tiled=True)]
    dot_general x4, local copies, waits for them, and re-layouts: 5.27 us -> 3.35 us  [tile_sum(): jnp.einsum('kij,kjf->kif', tiles, sources, preferred_element_type=jnp.flo...]
    eq x2, local copies, waits for them, and re-layouts: 1.72 us -> 0.01 us  [tile_sum(): rows[None, :] == jnp.arange(block_count, dtype=jnp.int32)[:, None]]
    gather x2, local copies, waits for them, and re-layouts: 2.78 us -> 1.16 us  [layer(): hub_sources = jnp.take(hub_blocks, hub_coord[:, 1], axis=0)]
  transfers between devices with their start and end apart: 2 -> 6, of which waited for: 0 -> 1; matrix products, arithmetic and copies ran while one was open for 22% -> 37% of each run, Pallas kernels for 0% -> 0%
where the time goes in v1:
time: 99.5 us; the launch traced here: 98.8 us
  matrix products  28.8 us (29%)
  local copies, waits for them, and re-layouts  25.3 us (25%)
  blocking collectives  19.9 us (20%)
  starting transfers between devices  12.7 us (13%)
  other arithmetic  5.73 us (6%)
  waiting for transfers between devices  5.27 us (5%)
  between operations  1.18 us (1%)
    all_gather x2, blocking collectives, layer(): inner = lax.all_gather(own_hubs, 'gy', axis=0, tiled=True)  19.9 us
    dot_general x6, matrix products, tile_sum(): merged = jnp.dot(onehot, flat, precision=lax.Precision.HIGHEST)  12.4 us
    dot_general x6, matrix products, tile_sum(): jnp.einsum('kij,kjf->kif', tiles, sources, preferred_element_type=jnp.flo...  12.1 us
    unnamed x32, local copies, waits for them, and re-layouts  11 us
    all_to_all x2, starting transfers between devices, layer(): lax.all_to_all(outgoing, 'gy', split_axis=0, concat_axis=0, tiled=True)  7.17 us
    ppermute x4, starting transfers between devices, layer(): lax.ppermute(line, 'gx', [(d, (d - have) % ways) for d in range(ways)])  5.51 us
    ppermute x4, waiting for transfers between devices, layer(): lax.ppermute(line, 'gx', [(d, (d - have) % ways) for d in range(ways)])  5.27 us
    gather x2, local copies, waits for them, and re-layouts, layer(): sources = jnp.take(blocks, local_coord[:, 1], axis=0)  4.04 us
  transfers between devices with their start and end apart: 6, of which 1 were waited for; matrix products, arithmetic and copies ran while one was open for 37% of the time, Pallas kernels for 0%

profile of v1, /device:TPU:0, one launch (start us, length us, event | category | flops | bytes accessed | tf_op | source)
XLA Modules:
  0.0 98.8 jit_solution(12717912374105884307)
XLA Ops:
  0.0 0.8 compare_select_fusion.1
  0.8 0.7 compare_and_fusion.1
  1.5 1.7 %gather_fusion.2 = bf16[8,256]{1,0:T(8,128)(2,1)S(1)} fusion(bf16[1024,256]{1,0:T(8,128)(2,1)} %param.25, s32[1024]{0:T(1024)S(1)} %pad_clamp_fusion.1), kind=kCustom, calls=%fused_computation.2.clone | custom fusion | bytes 8224 | tf_op jit(solution)/shard_map/jit(_take)/gather | solution.py:36
  3.2 10.5 %all_gather.6 = bf16[64,256]{1,0:T(8,128)(2,1)S(1)} all-gather(bf16[8,256]{1,0:T(8,128)(2,1)S(1)} %broadcast_select_fusion.3), channel_id=1, replica_groups=mesh['gx'=4,'gy'=8] {'gy'}, dimensions={0}, use_global_device_ids=true | all-gather | bytes 36864 | tf_op jit(solution)/shard_map/all_gather | solution.py:37
  13.8 3.6 %collective-permute-start = (bf16[64,256]{1,0:T(8,128)(2,1)S(1)}, bf16[64,256]{1,0:T(8,128)(2,1)S(1)}, u32[]{:S(2)}, u32[]{:S(2)}) collective-permute-start(bf16[64,256]{1,0:T(8,128)(2,1)S(1)} %all_gather.6), channel_id=1, source_target_pairs={{0,24},{8,0},{16,8},{24,16},{1,25},{9,1},{17,9},{25,17},{2,26},{10... | collective-permute-start | bytes 98312 | tf_op jit(solution)/shard_map/ppermute | solution.py:42
  17.4 1.7 %gather_fusion.1 = bf16[8,128,256]{2,1,0:T(8,128)(2,1)S(1)} fusion(bf16[8,128,256]{2,1,0:T(8,128)(2,1)} %bitcast.127, s32[1024]{0:T(1024)S(1)} %pad_clamp_fusion.2), kind=kCustom, calls=%fused_computation.1.clone | custom fusion | bytes 1048608 | tf_op jit(solution)/shard_map/jit(_take)/gather | solution.py:46
  19.0 0.3 copy.19
  19.3 0.9 broadcast_select_fusion.1
  20.2 3.5 %all-to-all-start = ((bf16[8,128,256]{1,2,0:T(8,128)(2,1)}), bf16[8,128,256]{1,2,0:T(8,128)(2,1)S(1)}, u32[]{:S(2)}, u32[]{:S(2)}) async-start(bf16[8,128,256]{1,2,0:T(8,128)(2,1)} %broadcast_select_fusion.1), calls=%async_computation | async-start | bytes 1048576 | tf_op jit(solution)/shard_map/all_to_all | solution.py:47
  23.8 2.0 %gather_fusion = bf16[32,128,256]{2,1,0:T(8,128)(2,1)} fusion(bf16[8,128,256]{2,1,0:T(8,128)(2,1)S(1)} %bitcast.128, s32[1024]{0:T(1024)S(1)} %pad_clamp_fusion.3), kind=kCustom, calls=%fused_computation.clone | custom fusion | bytes 4194432 | tf_op jit(solution)/shard_map/jit(_take)/gather | solution.py:51
  25.8 1.4 %fusion.74 = f32[1024,256]{1,0:T(8,128)} fusion(bf16[1024,256]{1,0:T(8,128)(2,1)S(1)} %copy-done.1, bf16[256,256]{1,0:T(8,128)(2,1)S(1)} %copy-done.8), kind=kOutput, calls=%fused_computation.125 | convolution fusion | flops 134217728 | bytes 1703936 | tf_op jit(solution)/shard_map/dot_general | solution.py:72
  27.2 4.4 %convolution_bitcast_fusion.1 = f32[32,128,256]{1,2,0:T(8,128)} fusion(bf16[32,128,128]{2,1,0:T(8,128)(2,1)S(1)} %copy-done, bf16[32,128,256]{2,1,0:T(8,128)(2,1)} %gather_fusion, pred[32]{0:T(512)(128)(4,1)S(1)} %get-tuple-element.10), kind=kOutput, calls=%fused_computation.15 | convolution fusion | flops 269484032 | bytes 7340064 | tf_op jit(solution)/shard_map/kij,kjf->kif/dot_general | solution.py:8
  31.7 5.4 %copy.38 = f32[4,8,128,256]{3,1,2,0:T(8,128)} copy(f32[4,8,128,256]{2,3,1,0:T(8,128)} %bitcast.129) | data formatting | bytes 8388608
  37.9 5.3 %collective-permute-done.1 = bf16[128,256]{1,0:T(8,128)(2,1)S(1)} collective-permute-done((bf16[128,256]{1,0:T(8,128)(2,1)S(1)}, bf16[128,256]{1,0:T(8,128)(2,1)S(1)}, u32[]{:S(2)}, u32[]{:S(2)}) %collective-permute-start.1) | collective-permute-done | bytes 65568 | tf_op jit(solution)/shard_map/ppermute | solution.py:42
  43.2 0.8 fusion.35
  44.0 0.6 gather_fusion.3
  44.6 1.4 %convolution_bitcast_fusion.4 = f32[8,128,256]{1,2,0:T(8,128)S(1)} fusion(bf16[8,128,128]{2,1,0:T(8,128)(2,1)} %param.38, bf16[8,128,256]{2,1,0:T(8,128)(2,1)S(1)} %gather_fusion.3, pred[8]{0:T(512)(128)(4,1)S(1)} %get-tuple-element.6), kind=kOutput, calls=%fused_computation.27 | convolution fusion | flops 67371008 | bytes 1835016 | tf_op jit(solution)/shard_map/kij,kjf->kif/dot_general | solution.py:8
  46.0 1.3 %copy.22 = f32[8,128,256]{2,1,0:T(8,128)} copy(f32[8,128,256]{1,2,0:T(8,128)S(1)} %convolution_bitcast_fusion.4) | data formatting | bytes 2097152 | tf_op jit(solution)/shard_map/kij,kjf->kif/dot_general | solution.py:8
  47.3 0.3 convolution_bitcast_fusion.5
  47.6 0.3 copy.20
  48.0 1.2 %fusion.45 = f32[8,128,256]{2,0,1:T(8,128)S(1)} fusion(s32[8]{0:T(128)S(1)} %copy-done.12, f32[1,8,128,256]{3,2,1,0:T(8,128)S(1)} %bitcast.131), kind=kOutput, calls=%fused_computation.88 | convolution fusion | flops 25165888 | bytes 2097184 | tf_op jit(solution)/shard_map/dot_general | solution.py:13
  49.2 3.8 %fusion.10 = f32[8,128,256]{2,0,1:T(8,128)S(1)} fusion(f32[8,128,256]{2,0,1:T(8,128)S(1)} %fusion.45, f32[32]{0:T(128)S(1)} %compare_convert_fusion, s32[32]{0:T(128)S(1)} %slice_bitcast_fusion.1, f32[4,8,128,256]{3,1,2,0:T(8,128)} %copy.38), kind=kOutput, calls=%fused_computation.20 | convolution fusion | flops 100925952 | bytes 6291712 | tf_op jit(solution)/shard_map/dot_general | solution.py:13
  53.0 1.2 %convolution_add_fusion.3 = f32[8,128,256]{2,0,1:T(8,128)S(1)} fusion(f32[8,128,256]{2,0,1:T(8,128)S(1)} %fusion.10, s32[8]{0:T(128)S(1)} %slice_bitcast_fusion, f32[1,8,128,256]{3,2,1,0:T(8,128)S(1)} %bitcast.134), kind=kOutput, calls=%fused_computation.30 | convolution fusion | flops 25428032 | bytes 3145760 | tf_op jit(solution)/shard_map/dot_general | solution.py:13
  54.2 0.3 copy.23
  54.8 0.4 multiply_reduce_fusion
  55.2 0.2 multiply_convert_fusion
  55.5 0.6 gather_fusion.6
  56.0 2.0 %gather_fusion.4 = bf16[32,128,256]{2,1,0:T(8,128)(2,1)} fusion(bf16[8,128,256]{2,1,0:T(8,128)(2,1)S(1)} %bitcast.125, s32[1024]{0:T(1024)S(1)} %pad_clamp_fusion.3), kind=kCustom, calls=%fused_computation.4.clone | custom fusion | bytes 4194432 | tf_op jit(solution)/shard_map/jit(_take)/gather | solution.py:51
  58.1 0.6 gather_fusion.5
  58.7 9.3 %all_gather.7 = bf16[64,256]{1,0:T(8,128)(2,1)S(1)} all-gather(bf16[8,256]{1,0:T(8,128)(2,1)S(1)} %broadcast_select_fusion.2), channel_id=1, replica_groups=mesh['gx'=4,'gy'=8] {'gy'}, dimensions={0}, use_global_device_ids=true | all-gather | bytes 36864 | tf_op jit(solution)/shard_map/all_gather | solution.py:37
  68.1 1.8 %collective-permute-start.2 = (bf16[64,256]{1,0:T(8,128)(2,1)S(1)}, bf16[64,256]{1,0:T(8,128)(2,1)S(1)}, u32[]{:S(2)}, u32[]{:S(2)}) collective-permute-start(bf16[64,256]{1,0:T(8,128)(2,1)S(1)} %all_gather.7), channel_id=1, source_target_pairs={{0,24},{8,0},{16,8},{24,16},{1,25},{9,1},{17,9},{25,17},{2,26},{10... | collective-permute-start | bytes 98312 | tf_op jit(solution)/shard_map/ppermute | solution.py:42
  69.8 4.4 %convolution_bitcast_fusion = f32[32,128,256]{1,2,0:T(8,128)} fusion(bf16[32,128,128]{2,1,0:T(8,128)(2,1)S(1)} %copy-done, bf16[32,128,256]{2,1,0:T(8,128)(2,1)} %gather_fusion.4, pred[32]{0:T(512)(128)(4,1)S(1)} %get-tuple-element.10), kind=kOutput, calls=%fused_computation.14 | convolution fusion | flops 269484032 | bytes 7340064 | tf_op jit(solution)/shard_map/kij,kjf->kif/dot_general | solution.py:8
  74.2 0.3 copy.27
  74.5 0.9 broadcast_select_fusion
  75.4 3.7 %all-to-all-start.1 = ((bf16[8,128,256]{1,2,0:T(8,128)(2,1)}), bf16[8,128,256]{1,2,0:T(8,128)(2,1)S(1)}, u32[]{:S(2)}, u32[]{:S(2)}) async-start(bf16[8,128,256]{1,2,0:T(8,128)(2,1)} %broadcast_select_fusion), calls=%async_computation.1 | async-start | bytes 1048576 | tf_op jit(solution)/shard_map/all_to_all | solution.py:47
  79.2 1.4 %fusion.75 = f32[1024,256]{1,0:T(8,128)} fusion(bf16[1024,256]{1,0:T(8,128)(2,1)S(1)} %multiply_convert_fusion, bf16[256,256]{1,0:T(8,128)(2,1)S(1)} %copy-done.9), kind=kOutput, calls=%fused_computation.126 | convolution fusion | flops 134217728 | bytes 1703936 | tf_op jit(solution)/shard_map/dot_general | solution.py:72
  80.6 5.5 %copy.41 = f32[4,8,128,256]{3,1,2,0:T(8,128)} copy(f32[4,8,128,256]{2,3,1,0:T(8,128)} %bitcast.130) | data formatting | bytes 8388608
  86.1 0.8 fusion.30
  86.9 0.6 gather_fusion.7
  87.5 1.4 %convolution_bitcast_fusion.2 = f32[8,128,256]{1,2,0:T(8,128)S(1)} fusion(bf16[8,128,128]{2,1,0:T(8,128)(2,1)} %param.38, bf16[8,128,256]{2,1,0:T(8,128)(2,1)S(1)} %gather_fusion.7, pred[8]{0:T(512)(128)(4,1)S(1)} %get-tuple-element.6), kind=kOutput, calls=%fused_computation.23 | convolution fusion | flops 67371008 | bytes 1835016 | tf_op jit(solution)/shard_map/kij,kjf->kif/dot_general | solution.py:8
  88.9 1.3 %copy.30 = f32[8,128,256]{2,1,0:T(8,128)} copy(f32[8,128,256]{1,2,0:T(8,128)S(1)} %convolution_bitcast_fusion.2) | data formatting | bytes 2097152 | tf_op jit(solution)/shard_map/kij,kjf->kif/dot_general | solution.py:8
  90.2 0.3 convolution_bitcast_fusion.3
  90.5 0.3 copy.28
  90.9 1.2 %fusion.43 = f32[8,128,256]{2,0,1:T(8,128)S(1)} fusion(s32[8]{0:T(128)S(1)} %copy-done.12, f32[1,8,128,256]{3,2,1,0:T(8,128)S(1)} %bitcast.132), kind=kOutput, calls=%fused_computation.87 | convolution fusion | flops 25165888 | bytes 2097184 | tf_op jit(solution)/shard_map/dot_general | solution.py:13
  92.0 3.8 %fusion.13 = f32[8,128,256]{2,0,1:T(8,128)S(1)} fusion(f32[8,128,256]{2,0,1:T(8,128)S(1)} %fusion.43, f32[32]{0:T(128)S(1)} %compare_convert_fusion, s32[32]{0:T(128)S(1)} %slice_bitcast_fusion.1, f32[4,8,128,256]{3,1,2,0:T(8,128)} %copy.41), kind=kOutput, calls=%fused_computation.21 | convolution fusion | flops 100925952 | bytes 6291712 | tf_op jit(solution)/shard_map/dot_general | solution.py:13
  95.9 1.2 %convolution_add_fusion.2 = f32[8,128,256]{2,0,1:T(8,128)S(1)} fusion(f32[8,128,256]{2,0,1:T(8,128)S(1)} %fusion.13, s32[8]{0:T(128)S(1)} %slice_bitcast_fusion, f32[1,8,128,256]{3,2,1,0:T(8,128)S(1)} %bitcast.133), kind=kOutput, calls=%fused_computation.29 | convolution fusion | flops 25428032 | bytes 3145760 | tf_op jit(solution)/shard_map/dot_general | solution.py:13
  97.1 0.3 copy.31
  97.7 1.1 %fusion.17 = bf16[1024,256]{1,0:T(8,128)(2,1)} fusion(f32[1024,256]{1,0:T(8,128)S(1)} %copy-done.5, bf16[1024,256]{1,0:T(8,128)(2,1)S(1)} %fusion.18, bf16[256,256]{1,0:T(8,128)(2,1)S(1)} %copy-done.7), kind=kOutput, calls=%fused_computation.31 | convolution fusion | flops 134742016 | bytes 2228224 | tf_op jit(solution)/shard_map/dot_general | solution.py:73
  (54 shorter events, 0.9 us)
Async XLA Ops:
  0.0 27.2 %copy-start = (bf16[32,128,128]{2,1,0:T(8,128)(2,1)S(1)}, bf16[32,128,128]{2,1,0:T(8,128)(2,1)}, u32[]{:S(2)}) copy-start(bf16[32,128,128]{2,1,0:T(8,128)(2,1)} %param.31) | copy-start | bytes 3145732
  0.0 23.8 %copy-start.1 = (bf16[1024,256]{1,0:T(8,128)(2,1)S(1)}, bf16[1024,256]{1,0:T(8,128)(2,1)}, u32[]{:S(2)}) copy-start(bf16[1024,256]{1,0:T(8,128)(2,1)} %param.25) | copy-start | bytes 1572868
  0.0 23.7 %copy-start.13 = (s32[32,2]{0,1:T(2,128)S(1)}, s32[32,2]{0,1:T(2,128)}, u32[]{:S(2)}) copy-start(s32[32,2]{0,1:T(2,128)} %param.32) | copy-start | bytes 772
  0.0 23.8 %copy-start.14 = (s32[8,2]{0,1:T(2,128)S(1)}, s32[8,2]{0,1:T(2,128)}, u32[]{:S(2)}) copy-start(s32[8,2]{0,1:T(2,128)} %param.39) | copy-start | bytes 196
  13.8 24.1 %collective-permute-start = (bf16[64,256]{1,0:T(8,128)(2,1)S(1)}, bf16[64,256]{1,0:T(8,128)(2,1)S(1)}, u32[]{:S(2)}, u32[]{:S(2)}) collective-permute-start(bf16[64,256]{1,0:T(8,128)(2,1)S(1)} %all_gather.6), channel_id=1, source_target_pairs={{0,24},{8,0},{16,8},{24,16},{1,25},{9,1},{17,9},{25,17},{2,26},{10... | collective-permute-start | bytes 98312 | tf_op jit(solution)/shard_map/ppermute | solution.py:42
  17.4 8.5 %copy-start.8 = (bf16[256,256]{1,0:T(8,128)(2,1)S(1)}, bf16[256,256]{1,0:T(8,128)(2,1)}, u32[]{:S(2)}) copy-start(bf16[256,256]{1,0:T(8,128)(2,1)} %param.26) | copy-start | bytes 393220
  20.2 27.1 %all-to-all-start = ((bf16[8,128,256]{1,2,0:T(8,128)(2,1)}), bf16[8,128,256]{1,2,0:T(8,128)(2,1)S(1)}, u32[]{:S(2)}, u32[]{:S(2)}) async-start(bf16[8,128,256]{1,2,0:T(8,128)(2,1)} %broadcast_select_fusion.1), calls=%async_computation | async-start | bytes 1048576 | tf_op jit(solution)/shard_map/all_to_all | solution.py:47
  31.7 6.1 %copy-start.11 = (s32[1024]{0:T(1024)S(1)}, s32[1024]{0:T(1024)}, u32[]{:S(2)}) copy-start(s32[1024]{0:T(1024)} %param.30) | copy-start | bytes 12292
  37.1 10.2 %copy-start.6 = (bf16[8,128,128]{2,1,0:T(8,128)(2,1)S(1)}, bf16[8,128,128]{2,1,0:T(8,128)(2,1)}, u32[]{:S(2)}) copy-start(bf16[8,128,128]{2,1,0:T(8,128)(2,1)} %param.35) | copy-start | bytes 786436
  37.9 5.4 %collective-permute-start.1 = (bf16[128,256]{1,0:T(8,128)(2,1)S(1)}, bf16[128,256]{1,0:T(8,128)(2,1)S(1)}, u32[]{:S(2)}, u32[]{:S(2)}) collective-permute-start(bf16[128,256]{1,0:T(8,128)(2,1)S(1)} %pad_maximum_fusion), channel_id=1, source_target_pairs={{0,16},{8,24},{16,0},{24,8},{1,17},{9,25},{17,1},{25,9},{2,18},{10... | collective-permute-start | bytes 196616 | tf_op jit(solution)/shard_map/ppermute | solution.py:42
  44.6 3.4 %copy-start.12 = (s32[8]{0:T(128)S(1)}, s32[8]{0:T(128)}, u32[]{:S(2)}) copy-start(s32[8]{0:T(128)} %param.36) | copy-start | bytes 100
  48.0 5.1 %copy-start.3 = (f32[8,128,256]{2,1,0:T(8,128)S(1)}, f32[8,128,256]{2,1,0:T(8,128)}, u32[]{:S(2)}) copy-start(f32[8,128,256]{2,1,0:T(8,128)} %copy.22) | copy-start | bytes 3145732
  53.0 1.8 %copy-start.4 = (f32[1024,256]{1,0:T(8,128)S(1)}, f32[1024,256]{1,0:T(8,128)}, u32[]{:S(2)}) copy-start(f32[1024,256]{1,0:T(8,128)} %fusion.74) | copy-start | bytes 3145732
  53.0 1.8 %copy-start.10 = (bf16[256,256]{1,0:T(8,128)(2,1)S(1)}, bf16[256,256]{1,0:T(8,128)(2,1)}, u32[]{:S(2)}) copy-start(bf16[256,256]{1,0:T(8,128)(2,1)} %param.27) | copy-start | bytes 393220
  68.1 11.1 %copy-start.9 = (bf16[256,256]{1,0:T(8,128)(2,1)S(1)}, bf16[256,256]{1,0:T(8,128)(2,1)}, u32[]{:S(2)}) copy-start(bf16[256,256]{1,0:T(8,128)(2,1)} %param.28) | copy-start | bytes 393220
  68.1 11.0 %collective-permute-start.2 = (bf16[64,256]{1,0:T(8,128)(2,1)S(1)}, bf16[64,256]{1,0:T(8,128)(2,1)S(1)}, u32[]{:S(2)}, u32[]{:S(2)}) collective-permute-start(bf16[64,256]{1,0:T(8,128)(2,1)S(1)} %all_gather.7), channel_id=1, source_target_pairs={{0,24},{8,0},{16,8},{24,16},{1,25},{9,1},{17,9},{25,17},{2,26},{10... | collective-permute-start | bytes 98312 | tf_op jit(solution)/shard_map/ppermute | solution.py:42
  75.4 14.8 %all-to-all-start.1 = ((bf16[8,128,256]{1,2,0:T(8,128)(2,1)}), bf16[8,128,256]{1,2,0:T(8,128)(2,1)S(1)}, u32[]{:S(2)}, u32[]{:S(2)}) async-start(bf16[8,128,256]{1,2,0:T(8,128)(2,1)} %broadcast_select_fusion), calls=%async_computation.1 | async-start | bytes 1048576 | tf_op jit(solution)/shard_map/all_to_all | solution.py:47
  79.1 7.0 %collective-permute-start.3 = (bf16[128,256]{1,0:T(8,128)(2,1)S(1)}, bf16[128,256]{1,0:T(8,128)(2,1)S(1)}, u32[]{:S(2)}, u32[]{:S(2)}) collective-permute-start(bf16[128,256]{1,0:T(8,128)(2,1)S(1)} %pad_maximum_fusion.1), channel_id=1, source_target_pairs={{0,16},{8,24},{16,0},{24,8},{1,17},{9,25},{17,1},{25,9},{2,18},{10... | collective-permute-start | bytes 196616 | tf_op jit(solution)/shard_map/ppermute | solution.py:42
  90.9 5.1 %copy-start.2 = (f32[8,128,256]{2,1,0:T(8,128)S(1)}, f32[8,128,256]{2,1,0:T(8,128)}, u32[]{:S(2)}) copy-start(f32[8,128,256]{2,1,0:T(8,128)} %copy.30) | copy-start | bytes 3145732
  95.9 1.8 %copy-start.5 = (f32[1024,256]{1,0:T(8,128)S(1)}, f32[1024,256]{1,0:T(8,128)}, u32[]{:S(2)}) copy-start(f32[1024,256]{1,0:T(8,128)} %fusion.75) | copy-start | bytes 3145732
  95.9 1.8 %copy-start.7 = (bf16[256,256]{1,0:T(8,128)(2,1)S(1)}, bf16[256,256]{1,0:T(8,128)(2,1)}, u32[]{:S(2)}) copy-start(bf16[256,256]{1,0:T(8,128)(2,1)} %param.29) | copy-start | bytes 393220
